TPU v7x, 32 devices: a whole 2x2x4 slice. The times are simulated.
32 devices in a mesh: section: 2 (over x), tile: 8 (over z, core), slide: 2 (over y).
Axes of the slice: x: 2, y: 2, z: 4, core: 2. Of those that a mesh axis runs over, the one named last changes fastest.
Arguments:
- features: bfloat16 [2, 16384, 2048], P('slide', ('section', 'tile')), may hold values from -6 to 6
- w_proj: bfloat16 [2048, 1024], P(('section', 'tile', 'slide')), may hold values from -0.25 to 0.25
- w_fc: bfloat16 [1024, 128], replicated, may hold values from -0.1875 to 0.1875
- w_up: bfloat16 [3, 128, 256], replicated, may hold values from -0.5 to 0.5
- w_down: bfloat16 [3, 256, 128], replicated, may hold values from -0.375 to 0.375
- self_adj: bfloat16 [2, 128, 128, 128], P('slide', ('section', 'tile')), may hold values from -0.1875 to 0.1875
- adjacency: bfloat16 [2, 128, 8, 128, 128], P('slide', ('section', 'tile')), may hold values from -0.1875 to 0.1875
- nbr_block: int32 [2, 128, 8], P('slide'), may hold values from 0 to 127, as said below
- counts: int32 [2, 128], P('slide', ('section', 'tile')), may hold values from 6 to 8
Outputs:
- node_out: bfloat16 [2, 16384, 128], P('slide', ('section', 'tile'))
Inputs may be any that keep to these rules, and one draw needn't show every extreme that they name: `nbr_block`: block g of a slide is the (g % 8)-th block of the (g // 8)-th group of 8 blocks. Among the 64 entries of one such group, at most 4 name blocks of any one group, and some group is named exactly 4 times; slots beyond counts are named too.
All inputs are finite; a program needn't handle non-finite values.
Results may differ from a plain program's by a relative error of at most 0.015.
Values may be sent and summed in bfloat16 or wider, within the bound.
A program may use at most 64 MiB of HBM per device.

v0:
```python
import jax
import jax.numpy as jnp
from jax import lax
from jax.sharding import PartitionSpec as P

HOPS = 3


def local(features, w_proj, w_fc, w_up, w_down, self_adj, adjacency, nbr_block, counts):
    rows = features[0]
    blocks = self_adj.shape[1]
    tb = self_adj.shape[2]
    width = w_fc.shape[1]
    slots = adjacency.shape[2]
    peers = lax.axis_size("section") * lax.axis_size("tile")
    me_index = lax.axis_index("section") * lax.axis_size("tile") + lax.axis_index("tile")
    sends = blocks * slots
    cap = (sends + peers - 1) // peers
    pre = jnp.dot(
        rows,
        lax.all_gather(w_proj, ("section", "tile", "slide"), axis=0, tiled=True),
        preferred_element_type=jnp.float32,
    )
    encoded = jax.nn.relu(pre).astype(jnp.bfloat16)
    state = jnp.dot(encoded, w_fc, preferred_element_type=jnp.float32)
    table = nbr_block[0].reshape(peers, sends)
    target_dev = table // blocks
    target_local = table % blocks
    positions = jnp.arange(sends, dtype=jnp.int32)
    before = positions[None, :] < positions[:, None]
    same = target_dev[:, :, None] == target_dev[:, None, :]
    ranking = jnp.sum(jnp.logical_and(same, before[None]).astype(jnp.int32), axis=2)
    mine_dev = lax.dynamic_index_in_dim(target_dev, me_index, 0, keepdims=False)
    mine_rank = lax.dynamic_index_in_dim(ranking, me_index, 0, keepdims=False)
    slot_of = mine_dev * cap + mine_rank
    send_map = (jnp.arange(peers * cap, dtype=jnp.int32)[:, None] == slot_of[None, :]).astype(
        jnp.bfloat16
    )
    arrive_hit = target_dev == me_index
    slot_flags = jnp.logical_and(
        arrive_hit[:, :, None],
        ranking[:, :, None] == jnp.arange(cap, dtype=jnp.int32)[None, None, :],
    ).astype(jnp.float32)
    local_flags = (
        target_local[:, :, None] == jnp.arange(blocks, dtype=jnp.int32)[None, None, :]
    ).astype(jnp.float32)
    recv_map = (
        jnp.einsum("pjc,pjr->rpc", slot_flags, local_flags)
        .reshape(blocks, peers * cap)
        .astype(jnp.bfloat16)
    )
    live = jnp.arange(slots, dtype=jnp.int32)[None, :] < counts[0][:, None]
    for hop in range(HOPS):
        nodes = state.astype(jnp.bfloat16).reshape(blocks, tb, width)
        own = jnp.einsum("bij,bjh->bih", self_adj[0], nodes, preferred_element_type=jnp.float32)
        terms = jnp.einsum(
            "bkij,bjh->bkih", adjacency[0], nodes, preferred_element_type=jnp.float32
        )
        terms = (
            jnp.where(live[:, :, None, None], terms, 0.0)
            .astype(jnp.bfloat16)
            .reshape(sends, tb * width)
        )
        outgoing = jnp.dot(send_map, terms, preferred_element_type=jnp.float32).astype(jnp.bfloat16)
        outgoing = outgoing.reshape(peers, cap, tb, width)
        arrived = lax.all_to_all(
            outgoing, ("section", "tile"), split_axis=0, concat_axis=0, tiled=True
        )
        arrived = arrived.reshape(peers * cap, tb * width)
        incoming = jnp.dot(recv_map, arrived, preferred_element_type=jnp.float32).reshape(
            blocks, tb, width
        )
        gathered = (own + incoming).astype(jnp.bfloat16).reshape(blocks * tb, width)
        inner = jax.nn.relu(
            jnp.dot(gathered, w_up[hop], preferred_element_type=jnp.float32)
        ).astype(jnp.bfloat16)
        state = state + jnp.dot(inner, w_down[hop], preferred_element_type=jnp.float32)
    return state.astype(jnp.bfloat16)[None]


def solution(mesh):
    return jax.shard_map(
        local,
        mesh=mesh,
        in_specs=(
            P("slide", ("section", "tile"), None),
            P(("section", "tile", "slide"), None),
            P(),
            P(),
            P(),
            P("slide", ("section", "tile"), None, None),
            P("slide", ("section", "tile"), None, None, None),
            P("slide", None, None),
            P("slide", ("section", "tile")),
        ),
        out_specs=P("slide", ("section", "tile"), None),
        check_vma=False,
    )
```

profile of v0, /device:TPU:0, one launch (start us, length us, event | category | flops | bytes accessed | tf_op | source)
XLA Modules:
  0.0 289.0 jit_solution(17965108515185727498)
XLA Ops:
  7.3 0.8 copy.35
  8.7 0.7 iota_compare_fusion.8
  9.4 65.4 %all-gather.2.cloned.1.call-done = bf16[2048,1024]{1,0:T(8,128)(2,1)} async-done(((bf16[64,1024]{1,0:T(8,128)(2,1)}), bf16[2048,1024]{1,0:T(8,128)(2,1)}) %all-gather.2.cloned.1.call-update) | async-done | bytes 4194320 | tf_op jit(solution)/shard_map/all_gather | solution.py:21
  74.8 8.6 %fusion.98 = (bf16[1024,128]{1,0:T(8,128)(2,1)S(1)}, f32[1024,128]{1,0:T(8,128)S(1)}) fusion(bf16[1024,128]{1,0:T(8,128)(2,1)} %param.11, bf16[2048,1024]{1,0:T(8,128)(2,1)} %all-gather.2.cloned.1.call-done, bf16[1,1024,2048]{2,1,0:T(8,128)(2,1)} %param.9), kind=kOutput, calls=%fused_computation.106 | convolution fusion | flops 4565630976 | bytes 9437184 | tf_op jit(solution)/shard_map/dot_general | solution.py:25
  83.5 2.3 fusion.22
  85.7 3.9 %copy.37 = bf16[8,8,128,128]{3,2,1,0:T(8,128)(2,1)} copy(bf16[8,8,128,128]{2,3,1,0:T(8,128)(2,1)} %fusion.22) | data formatting | bytes 4194304 | tf_op jit(solution)/shard_map/convert_element_type | solution.py:61
  89.6 3.3 %fusion.31 = bf16[8,8,128,128]{3,1,2,0:T(8,128)(2,1)S(1)} fusion(bf16[8,8,128,128]{3,2,1,0:T(8,128)(2,1)} %copy.37, s32[64]{0:T(128)S(1)} %add_bitcast_fusion), kind=kOutput, calls=%fused_computation.33 | convolution fusion | flops 135270400 | bytes 4194560 | tf_op jit(solution)/shard_map/dot_general | solution.py:64
  92.9 1.9 copy.70
  94.8 4.6 %all-to-all-start = ((bf16[16,4,128,128]{3,2,1,0:T(8,128)(2,1)}), bf16[16,4,128,128]{3,2,1,0:T(8,128)(2,1)}, u32[]{:S(2)}, u32[]{:S(2)}) async-start(bf16[16,4,128,128]{3,2,1,0:T(8,128)(2,1)} %bitcast.201), calls=%async_computation | async-start | bytes 4194304 | tf_op jit(solution)/shard_map/all_to_all | solution.py:66
  99.6 45.2 %all-to-all-done = bf16[16,4,128,128]{3,2,1,0:T(8,128)(2,1)} async-done(((bf16[16,4,128,128]{3,2,1,0:T(8,128)(2,1)}), bf16[16,4,128,128]{3,2,1,0:T(8,128)(2,1)}, u32[]{:S(2)}, u32[]{:S(2)}) %all-to-all-start) | async-done | bytes 2097184 | tf_op jit(solution)/shard_map/all_to_all | solution.py:66
  144.7 2.8 fusion.16
  147.8 2.2 fusion.101
  150.0 2.2 fusion.25
  152.3 3.9 %copy.42 = bf16[8,8,128,128]{3,2,1,0:T(8,128)(2,1)} copy(bf16[8,8,128,128]{2,3,1,0:T(8,128)(2,1)} %fusion.25) | data formatting | bytes 4194304 | tf_op jit(solution)/shard_map/convert_element_type | solution.py:61
  156.2 3.3 %fusion.34 = bf16[8,8,128,128]{3,1,2,0:T(8,128)(2,1)S(1)} fusion(bf16[8,8,128,128]{3,2,1,0:T(8,128)(2,1)} %copy.42, s32[64]{0:T(128)S(1)} %add_bitcast_fusion), kind=kOutput, calls=%fused_computation.34 | convolution fusion | flops 135270400 | bytes 4194560 | tf_op jit(solution)/shard_map/dot_general | solution.py:64
  160.0 53.7 %all_to_all.15 = bf16[16,4,128,128]{3,2,1,0:T(8,128)(2,1)S(1)} all-to-all(bf16[16,4,128,128]{3,2,1,0:T(8,128)(2,1)S(1)} %bitcast.202), channel_id=1, replica_groups=mesh['section'=2,'tile'=8,'slide'=2] {'section','tile'}, dimensions={0} | all-to-all | bytes 4194304 | tf_op jit(solution)/shard_map/all_to_all | solution.py:66
  213.7 1.2 fusion.13
  215.2 1.6 fusion.104
  216.9 2.3 fusion.28
  219.1 3.9 %copy.47 = bf16[8,8,128,128]{3,2,1,0:T(8,128)(2,1)} copy(bf16[8,8,128,128]{2,3,1,0:T(8,128)(2,1)} %fusion.28) | data formatting | bytes 4194304 | tf_op jit(solution)/shard_map/convert_element_type | solution.py:61
  223.0 3.3 %fusion.37 = bf16[8,8,128,128]{3,1,2,0:T(8,128)(2,1)S(1)} fusion(bf16[8,8,128,128]{3,2,1,0:T(8,128)(2,1)} %copy.47, s32[64]{0:T(128)S(1)} %add_bitcast_fusion), kind=kOutput, calls=%fused_computation.35 | convolution fusion | flops 135270400 | bytes 4194560 | tf_op jit(solution)/shard_map/dot_general | solution.py:64
  226.9 51.7 %all_to_all.16 = bf16[16,4,128,128]{3,2,1,0:T(8,128)(2,1)S(1)} all-to-all(bf16[16,4,128,128]{3,2,1,0:T(8,128)(2,1)S(1)} %bitcast.203), channel_id=1, replica_groups=mesh['section'=2,'tile'=8,'slide'=2] {'section','tile'}, dimensions={0} | all-to-all | bytes 4194304 | tf_op jit(solution)/shard_map/all_to_all | solution.py:66
  278.6 1.2 fusion.10
  280.0 2.1 fusion.59
  (18 shorter events, 3.4 us)
Async XLA Ops:
  6.5 76.9 %copy-start = (bf16[1,8,8,128,128]{4,3,2,1,0:T(8,128)(2,1)S(1)}, bf16[1,8,8,128,128]{4,3,2,1,0:T(8,128)(2,1)}, u32[]{:S(2)}) copy-start(bf16[1,8,8,128,128]{4,3,2,1,0:T(8,128)(2,1)} %param.15) | copy-start | bytes 6291460
  6.5 68.3 %all-gather.2.cloned.1.call-start = ((), (), s32[]{:S(2)}) async-start(), calls=%async_computation.3 | async-start | bytes 4325376 | tf_op jit(solution)/shard_map/all_gather | solution.py:21
  94.8 50.0 %all-to-all-start = ((bf16[16,4,128,128]{3,2,1,0:T(8,128)(2,1)}), bf16[16,4,128,128]{3,2,1,0:T(8,128)(2,1)}, u32[]{:S(2)}, u32[]{:S(2)}) async-start(bf16[16,4,128,128]{3,2,1,0:T(8,128)(2,1)} %bitcast.201), calls=%async_computation | async-start | bytes 4194304 | tf_op jit(solution)/shard_map/all_to_all | solution.py:66
  99.4 48.1 %copy-start.1 = (bf16[1,8,128,128]{3,2,1,0:T(8,128)(2,1)S(1)}, bf16[1,8,128,128]{3,2,1,0:T(8,128)(2,1)}, u32[]{:S(2)}) copy-start(bf16[1,8,128,128]{3,2,1,0:T(8,128)(2,1)} %param.14) | copy-start | bytes 786436
Sparse Core Ops, SparseCore 0:
  10.3 64.4 all-gather.1
where the time goes:
time: 290 us; the launch traced here: 289 us
  waiting for transfers between devices  111 us (38%)
  blocking collectives  105 us (36%)
  matrix products  37.2 us (13%)
  local copies, waits for them, and re-layouts  15.6 us (5%)
  between operations  13.5 us (5%)
  starting transfers between devices  4.62 us (2%)
    all_to_all x2, blocking collectives, local(): lax.all_to_all(outgoing, ('section', 'tile'), split_axis=0, concat_axis=0...  105 us
    all_gather x1, waiting for transfers between devices, local(): lax.all_gather(w_proj, ('section', 'tile', 'slide'), axis=0, tiled=True)  65.4 us
    all_to_all x1, waiting for transfers between devices, local(): lax.all_to_all(outgoing, ('section', 'tile'), split_axis=0, concat_axis=0...  45.2 us
    convert_element_type x3, local copies, waits for them, and re-layouts, local(): terms = jnp.where(live[:, :, None, None], terms, 0.0).astype(jnp.bfloat16...  11.7 us
    dot_general x3, matrix products, local(): jnp.dot(send_map, terms, preferred_element_type=jnp.float32)  9.77 us
    dot_general x1, matrix products, local(): state = jnp.dot(encoded, w_fc, preferred_element_type=jnp.float32)  8.63 us
    dot_general x3, matrix products, local(): jnp.einsum('bkij,bjh->bkih', adjacency[0], nodes, preferred_element_type=...  6.76 us
    dot_general x3, matrix products, local(): jnp.dot(inner, w_down[hop], preferred_element_type=jnp.float32)  5.96 us
  transfers between devices with their start and end apart: 2, of which 2 were waited for; matrix products, arithmetic and copies ran while one was open for 1% of the time, Pallas kernels for 0%

commit v1 on v0

v1 whole, which is shorter than its diff:
```python
import functools

import jax
import jax.numpy as jnp
from jax import lax
from jax.experimental import pallas as pl
from jax.experimental.pallas import tpu as pltpu
from jax.sharding import PartitionSpec as P

MESH = pl.DeviceIdType.MESH
CORES = 2
BF = jnp.bfloat16
F32 = jnp.float32


def remote(src, dst, send_sem, recv_sem, device):
    return pltpu.make_async_remote_copy(
        src_ref=src,
        dst_ref=dst,
        send_sem=send_sem,
        recv_sem=recv_sem,
        device_id=device,
        device_id_type=MESH,
    )


def near_first(count):
    order = [0]
    for step in range(1, count // 2 + 1):
        order += [step] if step == count - step else [step, count - step]
    return order


def greet(devices):
    barrier = pltpu.get_barrier_semaphore()
    for device in devices:
        pl.semaphore_signal(barrier, inc=1, device_id=device, device_id_type=MESH)
    return lambda: pl.semaphore_wait(barrier, len(devices))


def encode_kernel(tiles, x_ref, w_ref, fc_ref, out_ref, w_all, acc, z_s, z_r, xy_s, xy_r, dg_s, dg_r, pt_s, pt_r):
    zs = tiles // CORES
    rows = w_ref.shape[0]
    half = rows // 2
    sx = lax.axis_index("section")
    sy = lax.axis_index("slide")
    t = lax.axis_index("tile")
    z, c = t // CORES, t % CORES
    ox, oy, oc = 1 - sx, 1 - sy, 1 - c
    partner = {"tile": z * CORES + oc}
    xn, yn = {"section": ox}, {"slide": oy}

    def zdev(o):
        return {"tile": ((z + o) % zs) * CORES + c}

    def at(x, o, core, y, part=None):
        zz = (z + o) % zs
        start = ((x * tiles + zz * CORES + core) * 2 + y) * rows
        if part is None:
            return w_all.at[pl.ds(pl.multiple_of(start, rows), rows)]
        return w_all.at[pl.ds(pl.multiple_of(start + part * half, half), half)]

    started = []

    def go(src, dst, ss, rs, device):
        copy = remote(src, dst, ss, rs, device)
        copy.start()
        started.append(copy)

    def arrived(dst, ss, rs, device):
        remote(dst, dst, ss, rs, device).wait_recv()

    wait = greet([partner, xn, yn] + [zdev(o) for o in range(1, zs)])
    start = ((sx * tiles + t) * 2 + sy) * rows
    w_all[pl.ds(pl.multiple_of(start, rows), rows)] = w_ref[...]
    wait()

    order = near_first(zs)
    for o in order[1:]:
        go(w_ref, at(sx, 0, c, sy), z_s.at[o], z_r.at[o], zdev(o))

    def line(o):
        src = w_ref if o == 0 else at(sx, o, c, sy)
        if o:
            arrived(src, z_s.at[0], z_r.at[zs - o], zdev(o))
        here = at(sx, o, c, sy)
        go(src, here, xy_s.at[0, o], xy_r.at[0, o], xn)
        go(src, here, xy_s.at[1, o], xy_r.at[1, o], yn)
        go(src, here, pt_s.at[0, o], pt_r.at[0, o], partner)

    def cross(o):
        ref = at(ox, o, c, sy)
        arrived(ref, xy_s.at[0, o], xy_r.at[0, o], xn)
        part = at(ox, o, c, sy, 0)
        go(part, part, dg_s.at[0, o], dg_r.at[0, o], yn)
        go(ref, ref, pt_s.at[1, o], pt_r.at[1, o], partner)
        ref = at(sx, o, c, oy)
        arrived(ref, xy_s.at[1, o], xy_r.at[1, o], yn)
        part = at(sx, o, c, oy, 1)
        go(part, part, dg_s.at[1, o], dg_r.at[1, o], xn)
        go(ref, ref, pt_s.at[2, o], pt_r.at[2, o], partner)

    def corner(o):
        for k, device in enumerate((yn, xn)):
            part = at(ox, o, c, oy, k)
            arrived(part, dg_s.at[k, o], dg_r.at[k, o], device)
            go(part, part, pt_s.at[3 + k, o], pt_r.at[3 + k, o], partner)

    depth = CORES * 2 * rows

    def multiply(o, first):
        refs = [at(sx, o, oc, sy), at(ox, o, oc, sy), at(sx, o, oc, oy), at(ox, o, oc, oy, 0), at(ox, o, oc, oy, 1)]
        for k, ref in enumerate(refs):
            arrived(ref, pt_s.at[k, o], pt_r.at[k, o], partner)
        cols = [((x * zs) + (z + o) % zs) * depth for x in (sx, ox)]
        slabs = [pl.ds(pl.multiple_of(s, depth), depth) for s in cols]
        tall = x_ref.shape[0] // 4

        def body(i, carry):
            strip = pl.ds(pl.multiple_of(i * tall, tall), tall)
            total = jnp.dot(x_ref[strip, slabs[0]], w_all[slabs[0], :], preferred_element_type=F32)
            total += jnp.dot(x_ref[strip, slabs[1]], w_all[slabs[1], :], preferred_element_type=F32)
            acc[strip, :] = total if first else acc[strip, :] + total
            return carry

        lax.fori_loop(0, 4, body, 0)

    for step in range(zs + 3):
        if step < zs:
            line(order[step])
        if 0 <= step - 1 < zs:
            cross(order[step - 1])
        if 0 <= step - 2 < zs:
            corner(order[step - 2])
        if 0 <= step - 3 < zs:
            multiply(order[step - 3], step == 3)

    tall = x_ref.shape[0] // 4

    def finish(i, carry):
        strip = pl.ds(pl.multiple_of(i * tall, tall), tall)
        enc = jnp.maximum(acc[strip, :], 0.0).astype(BF)
        out_ref[strip, :] = jnp.dot(enc, fc_ref[...], preferred_element_type=F32)
        return carry

    lax.fori_loop(0, 4, finish, 0)
    for copy in started:
        copy.wait_send()


def encode(rows, w_proj, w_fc):
    tiles = lax.axis_size("tile")
    zs = tiles // CORES
    vmem = pl.BlockSpec(memory_space=pltpu.VMEM)
    dma = pltpu.SemaphoreType.DMA
    return pl.pallas_call(
        functools.partial(encode_kernel, tiles),
        out_shape=jax.ShapeDtypeStruct((rows.shape[0], w_fc.shape[1]), F32),
        in_specs=[vmem] * 3,
        out_specs=vmem,
        scratch_shapes=[
            pltpu.VMEM((rows.shape[1], w_proj.shape[1]), BF),
            pltpu.VMEM((rows.shape[0], w_proj.shape[1]), F32),
            dma((zs,)),
            dma((zs,)),
            dma((2, zs)),
            dma((2, zs)),
            dma((2, zs)),
            dma((2, zs)),
            dma((5, zs)),
            dma((5, zs)),
        ],
        compiler_params=pltpu.CompilerParams(
            collective_id=0, has_side_effects=True, vmem_limit_bytes=40 << 20
        ),
        name="encode",
    )(rows, w_proj, w_fc)


def hops_kernel(tiles, cap, list_ref, state_ref, adj_ref, self_ref, up_ref, down_ref, out_ref,
                state, terms, send0, own0, recv0, send1, recv1, send2, recv2, agg, s0, r0, s1, r1, s2, r2):
    hops = up_ref.shape[0]
    zs = tiles // CORES
    blocks, slots, tb, _ = adj_ref.shape
    width = state_ref.shape[1]
    sends = blocks * slots
    sx = lax.axis_index("section")
    t = lax.axis_index("tile")
    z, c = t // CORES, t % CORES
    ox, oc = 1 - sx, 1 - c
    partner = {"tile": z * CORES + oc}
    xn = {"section": ox}
    order = near_first(zs)
    order = order[:0:-1] + [0]

    def zdev(o):
        return {"tile": ((z + o) % zs) * CORES + c}

    wait = greet([partner, xn] + [zdev(o) for o in range(1, zs)])
    terms[sends] = jnp.zeros((tb, width), BF)
    state[...] = state_ref[...]

    for hop in range(hops):
        pending = []

        def go(src, dst, ss, rs, device):
            copy = remote(src, dst, ss, rs, device)
            copy.start()
            pending.append(copy)

        def term(b, carry):
            nodes = state[pl.ds(pl.multiple_of(b * tb, tb), tb), :].astype(BF)
            whole = jnp.dot(adj_ref[b].reshape(slots * tb, tb), nodes, preferred_element_type=F32)
            terms[pl.ds(b * slots, slots)] = whole.astype(BF).reshape(slots, tb, width)
            agg[pl.ds(pl.multiple_of(b * tb, tb), tb), :] = jnp.dot(self_ref[b], nodes, preferred_element_type=F32)
            return carry

        lax.fori_loop(0, blocks, term, 0)
        if hop == 0:
            wait()

        def sums(dst, x, o, core):
            first = ((x * zs + (z + o) % zs) * CORES + core) * blocks

            def body(r, carry):
                base = (first + r) * cap
                total = terms[list_ref[base]].astype(F32)
                for j in range(1, cap):
                    total += terms[list_ref[base + j]].astype(F32)
                dst[r] = total.astype(BF)
                return carry

            lax.fori_loop(0, blocks, body, 0)

        def chip(k, i):
            o = order[i]
            x = (ox, sx)[k]
            sums(send0.at[k, i], x, o, oc)
            go(send0.at[k, i], recv0.at[hop, k, i], s0.at[hop, k, i], r0.at[hop, k, i], partner)
            sums(own0.at[k, i], x, o, c)

        def pair(i):
            remote(recv0.at[hop, 0, i], recv0.at[hop, 0, i], s0.at[hop, 0, i], r0.at[hop, 0, i], partner).wait_recv()

            def body(r, carry):
                send1[i, r] = (own0[0, i, r].astype(F32) + recv0[hop, 0, i, r].astype(F32)).astype(BF)
                return carry

            lax.fori_loop(0, blocks, body, 0)
            go(send1.at[i], recv1.at[hop, i], s1.at[hop, i], r1.at[hop, i], xn)

        chip(0, 0)
        for i in range(1, zs):
            chip(0, i)
            pair(i - 1)
        chip(1, 0)
        pair(zs - 1)
        for i in range(1, zs):
            chip(1, i)

        for i in range(zs):
            remote(recv0.at[hop, 1, i], recv0.at[hop, 1, i], s0.at[hop, 1, i], r0.at[hop, 1, i], partner).wait_recv()
            remote(recv1.at[hop, i], recv1.at[hop, i], s1.at[hop, i], r1.at[hop, i], xn).wait_recv()
            o = order[i]

            def body(r, carry):
                total = own0[1, i, r].astype(F32) + recv0[hop, 1, i, r].astype(F32)
                total += recv1[hop, i, r].astype(F32)
                if o:
                    send2[o - 1, r] = total.astype(BF)
                else:
                    agg[pl.ds(pl.multiple_of(r * tb, tb), tb), :] += total
                return carry

            lax.fori_loop(0, blocks, body, 0)
            if o:
                go(send2.at[o - 1], recv2.at[hop, o - 1], s2.at[hop, o - 1], r2.at[hop, o - 1], zdev(o))
        for o in order[:-1]:
            remote(recv2.at[hop, o - 1], recv2.at[hop, o - 1], s2.at[hop, o - 1], r2.at[hop, o - 1], zdev(o)).wait_recv()

        def mlp(r, carry):
            strip = pl.ds(pl.multiple_of(r * 2 * tb, 2 * tb), 2 * tb)
            total = agg[strip, :]
            for o in range(1, zs):
                total += recv2[hop, o - 1, pl.ds(r * 2, 2)].astype(F32).reshape(2 * tb, width)
            inner = jnp.dot(total.astype(BF), up_ref[hop], preferred_element_type=F32)
            inner = jnp.maximum(inner, 0.0).astype(BF)
            after = state[strip, :] + jnp.dot(inner, down_ref[hop], preferred_element_type=F32)
            state[strip, :] = after
            if hop == hops - 1:
                out_ref[strip, :] = after.astype(BF)
            return carry

        lax.fori_loop(0, blocks // 2, mlp, 0)
        for copy in pending:
            copy.wait_send()


def graph(state, adjacency, self_adj, w_up, w_down, lists, cap):
    tiles = lax.axis_size("tile")
    zs = tiles // CORES
    blocks, slots, tb, _ = adjacency.shape
    width = state.shape[1]
    hops = w_up.shape[0]
    piece = (blocks, tb, width)
    vmem = pl.BlockSpec(memory_space=pltpu.VMEM)
    dma = pltpu.SemaphoreType.DMA
    return pl.pallas_call(
        functools.partial(hops_kernel, tiles, cap),
        out_shape=jax.ShapeDtypeStruct(state.shape, BF),
        in_specs=[pl.BlockSpec(memory_space=pltpu.SMEM)] + [vmem] * 5,
        out_specs=vmem,
        scratch_shapes=[
            pltpu.VMEM(state.shape, F32),
            pltpu.VMEM((blocks * slots + 1, tb, width), BF),
            pltpu.VMEM((2, zs) + piece, BF),
            pltpu.VMEM((2, zs) + piece, BF),
            pltpu.VMEM((hops, 2, zs) + piece, BF),
            pltpu.VMEM((zs,) + piece, BF),
            pltpu.VMEM((hops, zs) + piece, BF),
            pltpu.VMEM((zs - 1,) + piece, BF),
            pltpu.VMEM((hops, zs - 1) + piece, BF),
            pltpu.VMEM(state.shape, F32),
            dma((hops, 2, zs)),
            dma((hops, 2, zs)),
            dma((hops, zs)),
            dma((hops, zs)),
            dma((hops, zs)),
            dma((hops, zs)),
        ],
        compiler_params=pltpu.CompilerParams(
            collective_id=1, has_side_effects=True, vmem_limit_bytes=50 << 20
        ),
        name="hops",
    )(lists, state, adjacency, self_adj, w_up, w_down)


def entry_lists(targets, live, total_blocks, cap):
    sends = targets.shape[0]
    positions = jnp.arange(sends, dtype=jnp.int32)
    same = (targets[:, None] == targets[None, :]) & live[None, :] & (positions[None, :] < positions[:, None])
    rank = jnp.sum(same.astype(jnp.int32), axis=1)
    hit = (jnp.arange(total_blocks, dtype=jnp.int32)[:, None, None] == targets[None, None, :]) & live[None, None, :]
    hit = hit & (jnp.arange(cap, dtype=jnp.int32)[None, :, None] == rank[None, None, :])
    found = jnp.sum(jnp.where(hit, positions[None, None, :] - sends, 0), axis=2) + sends
    return found.reshape(total_blocks * cap)


def local(features, w_proj, w_fc, w_up, w_down, self_adj, adjacency, nbr_block, counts):
    rows = features[0]
    blocks = self_adj.shape[1]
    tb = self_adj.shape[2]
    width = w_fc.shape[1]
    slots = adjacency.shape[2]
    hops = w_up.shape[0]
    pairs = lax.axis_size("section") == 2 and lax.axis_size("tile") % CORES == 0
    peers = lax.axis_size("section") * lax.axis_size("tile")
    me_index = lax.axis_index("section") * lax.axis_size("tile") + lax.axis_index("tile")
    sends = blocks * slots
    cap = (sends + peers - 1) // peers
    if pairs and lax.axis_size("slide") == 2 and w_proj.shape[0] % 32 == 0:
        state = encode(rows, w_proj, w_fc)
    else:
        pre = jnp.dot(
            rows,
            lax.all_gather(w_proj, ("section", "tile", "slide"), axis=0, tiled=True),
            preferred_element_type=F32,
        )
        encoded = jax.nn.relu(pre).astype(BF)
        state = jnp.dot(encoded, w_fc, preferred_element_type=F32)
    live = jnp.arange(slots, dtype=jnp.int32)[None, :] < counts[0][:, None]
    if pairs and blocks <= CORES * cap:
        targets = lax.dynamic_slice_in_dim(nbr_block[0], me_index * blocks, blocks, 0).reshape(sends)
        lists = entry_lists(targets, live.reshape(sends), peers * blocks, cap)
        return graph(state, adjacency[0], self_adj[0], w_up, w_down, lists, cap)[None]
    table = nbr_block[0].reshape(peers, sends)
    target_dev = table // blocks
    target_local = table % blocks
    positions = jnp.arange(sends, dtype=jnp.int32)
    before = positions[None, :] < positions[:, None]
    same = target_dev[:, :, None] == target_dev[:, None, :]
    ranking = jnp.sum(jnp.logical_and(same, before[None]).astype(jnp.int32), axis=2)
    mine_dev = lax.dynamic_index_in_dim(target_dev, me_index, 0, keepdims=False)
    mine_rank = lax.dynamic_index_in_dim(ranking, me_index, 0, keepdims=False)
    slot_of = mine_dev * cap + mine_rank
    send_map = (jnp.arange(peers * cap, dtype=jnp.int32)[:, None] == slot_of[None, :]).astype(BF)
    arrive_hit = target_dev == me_index
    slot_flags = jnp.logical_and(
        arrive_hit[:, :, None],
        ranking[:, :, None] == jnp.arange(cap, dtype=jnp.int32)[None, None, :],
    ).astype(F32)
    local_flags = (
        target_local[:, :, None] == jnp.arange(blocks, dtype=jnp.int32)[None, None, :]
    ).astype(F32)
    recv_map = (
        jnp.einsum("pjc,pjr->rpc", slot_flags, local_flags).reshape(blocks, peers * cap).astype(BF)
    )
    for hop in range(hops):
        nodes = state.astype(BF).reshape(blocks, tb, width)
        own = jnp.einsum("bij,bjh->bih", self_adj[0], nodes, preferred_element_type=F32)
        terms = jnp.einsum("bkij,bjh->bkih", adjacency[0], nodes, preferred_element_type=F32)
        terms = (
            jnp.where(live[:, :, None, None], terms, 0.0).astype(BF).reshape(sends, tb * width)
        )
        outgoing = jnp.dot(send_map, terms, preferred_element_type=F32).astype(BF)
        outgoing = outgoing.reshape(peers, cap, tb, width)
        arrived = lax.all_to_all(
            outgoing, ("section", "tile"), split_axis=0, concat_axis=0, tiled=True
        )
        arrived = arrived.reshape(peers * cap, tb * width)
        incoming = jnp.dot(recv_map, arrived, preferred_element_type=F32).reshape(
            blocks, tb, width
        )
        gathered = (own + incoming).astype(BF).reshape(blocks * tb, width)
        inner = jax.nn.relu(jnp.dot(gathered, w_up[hop], preferred_element_type=F32)).astype(BF)
        state = state + jnp.dot(inner, w_down[hop], preferred_element_type=F32)
    return state.astype(BF)[None]


def solution(mesh):
    return jax.shard_map(
        local,
        mesh=mesh,
        in_specs=(
            P("slide", ("section", "tile"), None),
            P(("section", "tile", "slide"), None),
            P(),
            P(),
            P(),
            P("slide", ("section", "tile"), None, None),
            P("slide", ("section", "tile"), None, None, None),
            P("slide", None, None),
            P("slide", ("section", "tile")),
        ),
        out_specs=P("slide", ("section", "tile"), None),
        check_vma=False,
    )
```

time: 290 us -> 153 us (0.53)
  Pallas kernels: 0 us -> 147 us
  waiting for transfers between devices: 111 us -> 0 us
  blocking collectives: 105 us -> 0 us
  matrix products: 37.2 us -> 0 us
  between operations: 13.5 us -> 0.09 us
  local copies, waits for them, and re-layouts: 15.6 us -> 5.3 us
  starting transfers between devices: 4.62 us -> 0 us
    pallas_call x0 -> x2, Pallas kernels: none -> 147 us  [the longest x1 111 us: graph(): pl.pallas_call(functools.partial(hops_kernel, tiles, cap), out_shape=jax....]
    all_to_all x2 -> x0, blocking collectives: 105 us -> none  [local(): lax.all_to_all(outgoing, ('section', 'tile'), split_axis=0, concat_axis=0...]
    all_gather x1 -> x0, waiting for transfers between devices: 65.4 us -> none  [local(): lax.all_gather(w_proj, ('section', 'tile', 'slide'), axis=0, tiled=True)]
    all_to_all x1 -> x0, waiting for transfers between devices: 45.2 us -> none  [local(): lax.all_to_all(outgoing, ('section', 'tile'), split_axis=0, concat_axis=0...]
    dot_general x17 -> x0, matrix products: 37.2 us -> none  [the longest x3 9.77 us: local(): jnp.dot(send_map, terms, preferred_element_type=jnp.float32)]
    convert_element_type x3 -> x0, local copies, waits for them, and re-layouts: 11.7 us -> none  [local(): terms = jnp.where(live[:, :, None, None], terms, 0.0).astype(jnp.bfloat16...]
    all_to_all x1 -> x0, starting transfers between devices: 4.62 us -> none  [local(): lax.all_to_all(outgoing, ('section', 'tile'), split_axis=0, concat_axis=0...]
  transfers between devices with their start and end apart: 2 -> 0, of which waited for: 2 -> 0; matrix products, arithmetic and copies ran while one was open for 1% -> 0% of each run, Pallas kernels for 0% -> 0%
where the time goes in v1:
time: 153 us
  Pallas kernels  147 us (96%)
  local copies, waits for them, and re-layouts  5.3 us (3%)
    pallas_call x1, Pallas kernels, graph(): pl.pallas_call(functools.partial(hops_kernel, tiles, cap), out_shape=jax....  111 us
    pallas_call x1, Pallas kernels, encode(): pl.pallas_call(functools.partial(encode_kernel, tiles), out_shape=jax.Sha...  35.4 us
    unnamed x17, local copies, waits for them, and re-layouts  4.76 us

profile of v1, /device:TPU:0, one launch (start us, length us, event | category | flops | bytes accessed | tf_op | source)
XLA Modules:
  0.0 153.2 jit_solution(17200825015464898271)
XLA Ops:
  0.0 0.0 copy-start
  0.0 0.0 copy-start.5
  0.0 0.8 iota_compare_fusion.2
  0.8 0.1 lt.47
  0.9 0.0 copy-done
  0.9 0.1 constant_dynamic-slice_fusion
  0.9 0.1 copy.12
  1.0 0.1 eq.52
  1.1 0.2 convert_reduce_fusion
  1.3 0.1 fusion
  1.4 0.1 select_reduce_fusion
  1.5 0.1 copy.13
  1.6 0.1 add.26.list_ref
  1.8 0.0 copy-start.1
  1.8 2.2 %copy-done.1 = bf16[1,1024,2048]{2,1,0:T(8,128)(2,1)S(1)} copy-done((bf16[1,1024,2048]{2,1,0:T(8,128)(2,1)S(1)}, bf16[1,1024,2048]{2,1,0:T(8,128)(2,1)}, u32[]{:S(2)}) %copy-start.1) | copy-done | bytes 4194328
  3.9 0.9 copy-done.3
  4.9 0.9 copy-done.7
  5.8 35.4 %encode.1.state_ref = f32[1024,128]{1,0:T(8,128)S(1)} custom-call(bf16[1024,2048]{1,0:T(8,128)(2,1)S(1)} %bitcast.5, bf16[64,1024]{1,0:T(8,128)(2,1)S(1)} %copy-done.7, bf16[1024,128]{1,0:T(8,128)(2,1)S(1)} %copy-done.3), custom_call_target="tpu_custom_call" | custom-call | tf_op jit(solution)/shard_map/encode/pallas_call | solution.py:156
  41.2 0.0 copy-done.5
  41.2 0.0 copy-done.2
  41.2 0.0 copy-done.4
  41.2 0.0 copy-done.6
  41.2 111.3 %hops.1 = bf16[1024,128]{1,0:T(8,128)(2,1)S(1)} custom-call(s32[512]{0:T(512)S(1)} %add.26.list_ref, f32[1024,128]{1,0:T(8,128)S(1)} %encode.1.state_ref, bf16[8,8,128,128]{3,2,1,0:T(8,128)(2,1)S(1)} %bitcast.6, bf16[8,128,128]{2,1,0:T(8,128)(2,1)S(1)} %bitcast.8, bf16[3,128,256]{2,1,0:T(8,128)(2,1)S(1)} %copy-done.5, bf16[3,256,128]{2,1,0:T(8,128)(2,1)S(1)} %copy-done.6), custom_call_target="tpu_custom_call" | custom-call | tf_op jit(solution)/shard_map/hops/pallas_call | solution.py:308
  152.5 0.7 copy.15
  (8 shorter events, 0.0 us)
Async XLA Ops:
  0.0 0.9 copy-start
  0.0 41.2 %copy-start.5 = (bf16[3,128,256]{2,1,0:T(8,128)(2,1)S(1)}, bf16[3,128,256]{2,1,0:T(8,128)(2,1)}, u32[]{:S(2)}) copy-start(bf16[3,128,256]{2,1,0:T(8,128)(2,1)} %up_ref.1) | copy-start | bytes 589828
  1.8 2.2 %copy-start.1 = (bf16[1,1024,2048]{2,1,0:T(8,128)(2,1)S(1)}, bf16[1,1024,2048]{2,1,0:T(8,128)(2,1)}, u32[]{:S(2)}) copy-start(bf16[1,1024,2048]{2,1,0:T(8,128)(2,1)} %param.9) | copy-start | bytes 12582916
  3.9 0.9 copy-start.3
  4.9 0.9 copy-start.7
  5.8 35.4 %copy-start.2 = (bf16[1,8,8,128,128]{4,3,2,1,0:T(8,128)(2,1)S(1)}, bf16[1,8,8,128,128]{4,3,2,1,0:T(8,128)(2,1)}, u32[]{:S(2)}) copy-start(bf16[1,8,8,128,128]{4,3,2,1,0:T(8,128)(2,1)} %param.15) | copy-start | bytes 6291460
  5.8 35.4 %copy-start.4 = (bf16[1,8,128,128]{3,2,1,0:T(8,128)(2,1)S(1)}, bf16[1,8,128,128]{3,2,1,0:T(8,128)(2,1)}, u32[]{:S(2)}) copy-start(bf16[1,8,128,128]{3,2,1,0:T(8,128)(2,1)} %param.14) | copy-start | bytes 786436
  5.8 35.4 %copy-start.6 = (bf16[3,256,128]{2,1,0:T(8,128)(2,1)S(1)}, bf16[3,256,128]{2,1,0:T(8,128)(2,1)}, u32[]{:S(2)}) copy-start(bf16[3,256,128]{2,1,0:T(8,128)(2,1)} %down_ref.1) | copy-start | bytes 589828

commit v2 on v1

--- a/solution.py
+++ b/solution.py
@@ -9,6 +9,7 @@
 
 MESH = pl.DeviceIdType.MESH
 CORES = 2
+PARTS = 2
 BF = jnp.bfloat16
 F32 = jnp.float32
 
@@ -38,7 +39,7 @@
     return lambda: pl.semaphore_wait(barrier, len(devices))
 
 
-def encode_kernel(tiles, x_ref, w_ref, fc_ref, out_ref, w_all, acc, z_s, z_r, xy_s, xy_r, dg_s, dg_r, pt_s, pt_r):
+def encode_kernel(tiles, x_hbm, w_ref, fc_hbm, out_ref, x_ref, fc_ref, w_all, acc, ld, z_s, z_r, xy_s, xy_r, dg_s, dg_r, pt_s, pt_r):
     zs = tiles // CORES
     rows = w_ref.shape[0]
     half = rows // 2
@@ -70,6 +71,9 @@
     def arrived(dst, ss, rs, device):
         remote(dst, dst, ss, rs, device).wait_recv()
 
+    loads = [pltpu.make_async_copy(x_hbm, x_ref, ld.at[0]), pltpu.make_async_copy(fc_hbm, fc_ref, ld.at[1])]
+    for load in loads:
+        load.start()
     wait = greet([partner, xn, yn] + [zdev(o) for o in range(1, zs)])
     start = ((sx * tiles + t) * 2 + sy) * rows
     w_all[pl.ds(pl.multiple_of(start, rows), rows)] = w_ref[...]
@@ -132,10 +136,13 @@
             cross(order[step - 1])
         if 0 <= step - 2 < zs:
             corner(order[step - 2])
+        if step == 3:
+            loads[0].wait()
         if 0 <= step - 3 < zs:
             multiply(order[step - 3], step == 3)
 
     tall = x_ref.shape[0] // 4
+    loads[1].wait()
 
     def finish(i, carry):
         strip = pl.ds(pl.multiple_of(i * tall, tall), tall)
@@ -152,15 +159,19 @@
     tiles = lax.axis_size("tile")
     zs = tiles // CORES
     vmem = pl.BlockSpec(memory_space=pltpu.VMEM)
+    hbm = pl.BlockSpec(memory_space=pltpu.HBM)
     dma = pltpu.SemaphoreType.DMA
     return pl.pallas_call(
         functools.partial(encode_kernel, tiles),
         out_shape=jax.ShapeDtypeStruct((rows.shape[0], w_fc.shape[1]), F32),
-        in_specs=[vmem] * 3,
+        in_specs=[hbm, vmem, hbm],
         out_specs=vmem,
         scratch_shapes=[
+            pltpu.VMEM(rows.shape, BF),
+            pltpu.VMEM(w_fc.shape, BF),
             pltpu.VMEM((rows.shape[1], w_proj.shape[1]), BF),
             pltpu.VMEM((rows.shape[0], w_proj.shape[1]), F32),
+            dma((2,)),
             dma((zs,)),
             dma((zs,)),
             dma((2, zs)),
@@ -177,28 +188,47 @@
     )(rows, w_proj, w_fc)
 
 
-def hops_kernel(tiles, cap, list_ref, state_ref, adj_ref, self_ref, up_ref, down_ref, out_ref,
-                state, terms, send0, own0, recv0, send1, recv1, send2, recv2, agg, s0, r0, s1, r1, s2, r2):
+def hops_kernel(tiles, cap, parts, list_ref, state_ref, adj_ref, self_ref, up_ref, down_ref, out_ref,
+                state, terms, send0, own0, recv0, send1, recv1, send2, recv2, send3, recv3, agg,
+                s0, r0, s1, r1, s2, r2, s3, r3):
     hops = up_ref.shape[0]
     zs = tiles // CORES
+    far = zs // 2
     blocks, slots, tb, _ = adj_ref.shape
     width = state_ref.shape[1]
     sends = blocks * slots
+    per = blocks // parts
+    chunks = zs * parts
     sx = lax.axis_index("section")
     t = lax.axis_index("tile")
     z, c = t // CORES, t % CORES
     ox, oc = 1 - sx, 1 - c
+    oz = z + 1 - 2 * (z % 2)
     partner = {"tile": z * CORES + oc}
     xn = {"section": ox}
-    order = near_first(zs)
-    order = order[:0:-1] + [0]
-
-    def zdev(o):
-        return {"tile": ((z + o) % zs) * CORES + c}
-
-    wait = greet([partner, xn] + [zdev(o) for o in range(1, zs)])
+    zn = {"tile": oz * CORES + c}
+
+    def zdev(j):
+        return {"tile": ((z + 2 * j) % zs) * CORES + c}
+
+    order = []
+    for j in range(1, far):
+        order += [(oz + 2 * j) % zs, (z + 2 * j) % zs]
+    order += [oz, z]
+
+    wait = greet([partner, xn, zn] + [zdev(j) for j in range(1, far)])
     terms[sends] = jnp.zeros((tb, width), BF)
     state[...] = state_ref[...]
+
+    def term(b, carry):
+        nodes = state[pl.ds(pl.multiple_of(b * tb, tb), tb), :].astype(BF)
+        whole = jnp.dot(adj_ref[b].reshape(slots * tb, tb), nodes, preferred_element_type=F32)
+        terms[pl.ds(b * slots, slots)] = whole.astype(BF).reshape(slots, tb, width)
+        agg[pl.ds(pl.multiple_of(b * tb, tb), tb), :] = jnp.dot(self_ref[b], nodes, preferred_element_type=F32)
+        return carry
+
+    lax.fori_loop(0, blocks, term, 0)
+    wait()
 
     for hop in range(hops):
         pending = []
@@ -208,19 +238,12 @@
             copy.start()
             pending.append(copy)
 
-        def term(b, carry):
-            nodes = state[pl.ds(pl.multiple_of(b * tb, tb), tb), :].astype(BF)
-            whole = jnp.dot(adj_ref[b].reshape(slots * tb, tb), nodes, preferred_element_type=F32)
-            terms[pl.ds(b * slots, slots)] = whole.astype(BF).reshape(slots, tb, width)
-            agg[pl.ds(pl.multiple_of(b * tb, tb), tb), :] = jnp.dot(self_ref[b], nodes, preferred_element_type=F32)
-            return carry
-
-        lax.fori_loop(0, blocks, term, 0)
-        if hop == 0:
-            wait()
-
-        def sums(dst, x, o, core):
-            first = ((x * zs + (z + o) % zs) * CORES + core) * blocks
+        def arrived(dst, ss, rs, device):
+            remote(dst, dst, ss, rs, device).wait_recv()
+
+        def sums(dst, x, q, core):
+            i, h = divmod(q, parts)
+            first = ((x * zs + order[i]) * CORES + core) * blocks + h * per
 
             def body(r, carry):
                 base = (first + r) * cap
@@ -230,68 +253,82 @@
                 dst[r] = total.astype(BF)
                 return carry
 
-            lax.fori_loop(0, blocks, body, 0)
-
-        def chip(k, i):
-            o = order[i]
+            lax.fori_loop(0, per, body, 0)
+
+        def chip(k, q):
             x = (ox, sx)[k]
-            sums(send0.at[k, i], x, o, oc)
-            go(send0.at[k, i], recv0.at[hop, k, i], s0.at[hop, k, i], r0.at[hop, k, i], partner)
-            sums(own0.at[k, i], x, o, c)
-
-        def pair(i):
-            remote(recv0.at[hop, 0, i], recv0.at[hop, 0, i], s0.at[hop, 0, i], r0.at[hop, 0, i], partner).wait_recv()
+            sums(send0.at[k, q], x, q, oc)
+            go(send0.at[k, q], recv0.at[hop, k, q], s0.at[hop, k, q], r0.at[hop, k, q], partner)
+            sums(own0.at[k, q], x, q, c)
+
+        def pair(q):
+            arrived(recv0.at[hop, 0, q], s0.at[hop, 0, q], r0.at[hop, 0, q], partner)
 
             def body(r, carry):
-                send1[i, r] = (own0[0, i, r].astype(F32) + recv0[hop, 0, i, r].astype(F32)).astype(BF)
+                send1[q, r] = (own0[0, q, r].astype(F32) + recv0[hop, 0, q, r].astype(F32)).astype(BF)
                 return carry
 
-            lax.fori_loop(0, blocks, body, 0)
-            go(send1.at[i], recv1.at[hop, i], s1.at[hop, i], r1.at[hop, i], xn)
+            lax.fori_loop(0, per, body, 0)
+            go(send1.at[q], recv1.at[hop, q], s1.at[hop, q], r1.at[hop, q], xn)
 
         chip(0, 0)
-        for i in range(1, zs):
-            chip(0, i)
-            pair(i - 1)
+        for q in range(1, chunks):
+            chip(0, q)
+            pair(q - 1)
         chip(1, 0)
-        pair(zs - 1)
-        for i in range(1, zs):
-            chip(1, i)
-
-        for i in range(zs):
-            remote(recv0.at[hop, 1, i], recv0.at[hop, 1, i], s0.at[hop, 1, i], r0.at[hop, 1, i], partner).wait_recv()
-            remote(recv1.at[hop, i], recv1.at[hop, i], s1.at[hop, i], r1.at[hop, i], xn).wait_recv()
-            o = order[i]
-
-            def body(r, carry):
-                total = own0[1, i, r].astype(F32) + recv0[hop, 1, i, r].astype(F32)
-                total += recv1[hop, i, r].astype(F32)
-                if o:
-                    send2[o - 1, r] = total.astype(BF)
+        pair(chunks - 1)
+        for q in range(1, chunks):
+            chip(1, q)
+
+        for q in range(chunks):
+            i, h = divmod(q, parts)
+            arrived(recv0.at[hop, 1, q], s0.at[hop, 1, q], r0.at[hop, 1, q], partner)
+            arrived(recv1.at[hop, q], s1.at[hop, q], r1.at[hop, q], xn)
+            slot = (i // 2) * parts + h
+            onward = i % 2 == 0
+            if not onward:
+                arrived(recv2.at[hop, slot], s2.at[hop, slot], r2.at[hop, slot], zn)
+            home = i == zs - 1
+
+            def gathered(r):
+                total = own0[1, q, r].astype(F32) + recv0[hop, 1, q, r].astype(F32)
+                total += recv1[hop, q, r].astype(F32)
+                return total if onward else total + recv2[hop, slot, r].astype(F32)
+
+            if not home:
+                out = send2 if onward else send3
+
+                def body(r, carry):
+                    out[slot, r] = gathered(r).astype(BF)
+                    return carry
+
+                lax.fori_loop(0, per, body, 0)
+                if onward:
+                    go(send2.at[slot], recv2.at[hop, slot], s2.at[hop, slot], r2.at[hop, slot], zn)
                 else:
-                    agg[pl.ds(pl.multiple_of(r * tb, tb), tb), :] += total
+                    go(send3.at[slot], recv3.at[hop, slot], s3.at[hop, slot], r3.at[hop, slot], zdev(i // 2 + 1))
+                continue
+            for j in range(1, far):
+                there = (j - 1) * parts + h
+                arrived(recv3.at[hop, there], s3.at[hop, there], r3.at[hop, there], zdev(j))
+
+            def finish(r, carry):
+                rows = pl.ds(pl.multiple_of((h * per + r) * tb, tb), tb)
+                total = agg[rows, :] + gathered(r)
+                for j in range(1, far):
+                    total += recv3[hop, (j - 1) * parts + h, r].astype(F32)
+                inner = jnp.dot(total.astype(BF), up_ref[hop], preferred_element_type=F32)
+                inner = jnp.maximum(inner, 0.0).astype(BF)
+                after = state[rows, :] + jnp.dot(inner, down_ref[hop], preferred_element_type=F32)
+                if hop == hops - 1:
+                    out_ref[rows, :] = after.astype(BF)
+                else:
+                    state[rows, :] = after
                 return carry
 
-            lax.fori_loop(0, blocks, body, 0)
-            if o:
-                go(send2.at[o - 1], recv2.at[hop, o - 1], s2.at[hop, o - 1], r2.at[hop, o - 1], zdev(o))
-        for o in order[:-1]:
-            remote(recv2.at[hop, o - 1], recv2.at[hop, o - 1], s2.at[hop, o - 1], r2.at[hop, o - 1], zdev(o)).wait_recv()
-
-        def mlp(r, carry):
-            strip = pl.ds(pl.multiple_of(r * 2 * tb, 2 * tb), 2 * tb)
-            total = agg[strip, :]
-            for o in range(1, zs):
-                total += recv2[hop, o - 1, pl.ds(r * 2, 2)].astype(F32).reshape(2 * tb, width)
-            inner = jnp.dot(total.astype(BF), up_ref[hop], preferred_element_type=F32)
-            inner = jnp.maximum(inner, 0.0).astype(BF)
-            after = state[strip, :] + jnp.dot(inner, down_ref[hop], preferred_element_type=F32)
-            state[strip, :] = after
-            if hop == hops - 1:
-                out_ref[strip, :] = after.astype(BF)
-            return carry
-
-        lax.fori_loop(0, blocks // 2, mlp, 0)
+            lax.fori_loop(0, per, finish, 0, unroll=True)
+            if hop < hops - 1:
+                lax.fori_loop(h * per, h * per + per, term, 0)
         for copy in pending:
             copy.wait_send()
 
@@ -299,35 +336,40 @@
 def graph(state, adjacency, self_adj, w_up, w_down, lists, cap):
     tiles = lax.axis_size("tile")
     zs = tiles // CORES
+    far = zs // 2
     blocks, slots, tb, _ = adjacency.shape
     width = state.shape[1]
     hops = w_up.shape[0]
-    piece = (blocks, tb, width)
+    parts = PARTS if blocks % PARTS == 0 else 1
+    piece = (blocks // parts, tb, width)
+    chunks = zs * parts
+    onward = far * parts
+    distant = max(1, (far - 1) * parts)
     vmem = pl.BlockSpec(memory_space=pltpu.VMEM)
     dma = pltpu.SemaphoreType.DMA
     return pl.pallas_call(
-        functools.partial(hops_kernel, tiles, cap),
+        functools.partial(hops_kernel, tiles, cap, parts),
         out_shape=jax.ShapeDtypeStruct(state.shape, BF),
         in_specs=[pl.BlockSpec(memory_space=pltpu.SMEM)] + [vmem] * 5,
         out_specs=vmem,
         scratch_shapes=[
             pltpu.VMEM(state.shape, F32),
             pltpu.VMEM((blocks * slots + 1, tb, width), BF),
-            pltpu.VMEM((2, zs) + piece, BF),
-            pltpu.VMEM((2, zs) + piece, BF),
-            pltpu.VMEM((hops, 2, zs) + piece, BF),
-            pltpu.VMEM((zs,) + piece, BF),
-            pltpu.VMEM((hops, zs) + piece, BF),
-            pltpu.VMEM((zs - 1,) + piece, BF),
-            pltpu.VMEM((hops, zs - 1) + piece, BF),
+            pltpu.VMEM((2, chunks) + piece, BF),
+            pltpu.VMEM((2, chunks) + piece, BF),
+            pltpu.VMEM((hops, 2, chunks) + piece, BF),
+            pltpu.VMEM((chunks,) + piece, BF),
+            pltpu.VMEM((hops, chunks) + piece, BF),
+            pltpu.VMEM((onward,) + piece, BF),
+            pltpu.VMEM((hops, onward) + piece, BF),
+            pltpu.VMEM((distant,) + piece, BF),
+            pltpu.VMEM((hops, distant) + piece, BF),
             pltpu.VMEM(state.shape, F32),
-            dma((hops, 2, zs)),
-            dma((hops, 2, zs)),
-            dma((hops, zs)),
-            dma((hops, zs)),
-            dma((hops, zs)),
-            dma((hops, zs)),
-        ],
+        ]
+        + [dma((hops, 2, chunks))] * 2
+        + [dma((hops, chunks))] * 2
+        + [dma((hops, onward))] * 2
+        + [dma((hops, distant))] * 2,
         compiler_params=pltpu.CompilerParams(
             collective_id=1, has_side_effects=True, vmem_limit_bytes=50 << 20
         ),
@@ -353,7 +395,7 @@
     width = w_fc.shape[1]
     slots = adjacency.shape[2]
     hops = w_up.shape[0]
-    pairs = lax.axis_size("section") == 2 and lax.axis_size("tile") % CORES == 0
+    pairs = lax.axis_size("section") == 2 and lax.axis_size("tile") % (2 * CORES) == 0
     peers = lax.axis_size("section") * lax.axis_size("tile")
     me_index = lax.axis_index("section") * lax.axis_size("tile") + lax.axis_index("tile")
     sends = blocks * slots

time: 153 us -> 134 us (0.88)
  Pallas kernels: 147 us -> 127 us
    pallas_call x1, Pallas kernels: 111 us -> 91.7 us  [graph(): pl.pallas_call(functools.partial(hops_kernel, tiles, cap, parts), out_sha...]
where the time goes in v2:
time: 134 us
  Pallas kernels  127 us (95%)
  local copies, waits for them, and re-layouts  5.3 us (4%)
    pallas_call x1, Pallas kernels, graph(): pl.pallas_call(functools.partial(hops_kernel, tiles, cap, parts), out_sha...  91.7 us
    pallas_call x1, Pallas kernels, encode(): pl.pallas_call(functools.partial(encode_kernel, tiles), out_shape=jax.Sha...  35.7 us
    unnamed x17, local copies, waits for them, and re-layouts  4.76 us

profile of v2, /device:TPU:0, one launch (start us, length us, event | category | flops | bytes accessed | tf_op | source)
XLA Modules:
  0.0 134.0 jit_solution(7327125222885765529)
XLA Ops:
  0.0 0.0 copy-start
  0.0 0.0 copy-start.5
  0.0 0.8 iota_compare_fusion.2
  0.8 0.1 lt.47
  0.9 0.0 copy-done
  0.9 0.1 constant_dynamic-slice_fusion
  0.9 0.1 copy.12
  1.0 0.1 eq.52
  1.1 0.2 convert_reduce_fusion
  1.3 0.1 fusion
  1.4 0.1 select_reduce_fusion
  1.5 0.1 copy.13
  1.6 0.1 add.26.list_ref
  1.8 0.0 copy-start.1
  1.8 2.2 %copy-done.1 = bf16[1,1024,2048]{2,1,0:T(8,128)(2,1)S(1)} copy-done((bf16[1,1024,2048]{2,1,0:T(8,128)(2,1)S(1)}, bf16[1,1024,2048]{2,1,0:T(8,128)(2,1)}, u32[]{:S(2)}) %copy-start.1) | copy-done | bytes 4194328
  3.9 0.9 copy-done.3
  4.9 0.9 copy-done.7
  5.8 35.7 %encode.1.state_ref = f32[1024,128]{1,0:T(8,128)S(1)} custom-call(bf16[1024,2048]{1,0:T(8,128)(2,1)S(1)} %bitcast.5, bf16[64,1024]{1,0:T(8,128)(2,1)S(1)} %copy-done.7, bf16[1024,128]{1,0:T(8,128)(2,1)S(1)} %copy-done.3), custom_call_target="tpu_custom_call" | custom-call | tf_op jit(solution)/shard_map/encode/pallas_call | solution.py:164
  41.5 0.0 copy-done.5
  41.5 0.0 copy-done.2
  41.5 0.0 copy-done.4
  41.5 0.0 copy-done.6
  41.5 91.7 %hops.1 = bf16[1024,128]{1,0:T(8,128)(2,1)S(1)} custom-call(s32[512]{0:T(512)S(1)} %add.26.list_ref, f32[1024,128]{1,0:T(8,128)S(1)} %encode.1.state_ref, bf16[8,8,128,128]{3,2,1,0:T(8,128)(2,1)S(1)} %bitcast.6, bf16[8,128,128]{2,1,0:T(8,128)(2,1)S(1)} %bitcast.8, bf16[3,128,256]{2,1,0:T(8,128)(2,1)S(1)} %copy-done.5, bf16[3,256,128]{2,1,0:T(8,128)(2,1)S(1)} %copy-done.6), custom_call_target="tpu_custom_call" | custom-call | tf_op jit(solution)/shard_map/hops/pallas_call | solution.py:350
  133.3 0.7 copy.15
  (8 shorter events, 0.0 us)
Async XLA Ops:
  0.0 0.9 copy-start
  0.0 41.5 %copy-start.5 = (bf16[3,128,256]{2,1,0:T(8,128)(2,1)S(1)}, bf16[3,128,256]{2,1,0:T(8,128)(2,1)}, u32[]{:S(2)}) copy-start(bf16[3,128,256]{2,1,0:T(8,128)(2,1)} %up_ref.1) | copy-start | bytes 589828
  1.8 2.2 %copy-start.1 = (bf16[1,1024,2048]{2,1,0:T(8,128)(2,1)S(1)}, bf16[1,1024,2048]{2,1,0:T(8,128)(2,1)}, u32[]{:S(2)}) copy-start(bf16[1,1024,2048]{2,1,0:T(8,128)(2,1)} %param.9) | copy-start | bytes 12582916
  3.9 0.9 copy-start.3
  4.9 0.9 copy-start.7
  5.8 35.7 %copy-start.2 = (bf16[1,8,8,128,128]{4,3,2,1,0:T(8,128)(2,1)S(1)}, bf16[1,8,8,128,128]{4,3,2,1,0:T(8,128)(2,1)}, u32[]{:S(2)}) copy-start(bf16[1,8,8,128,128]{4,3,2,1,0:T(8,128)(2,1)} %param.15) | copy-start | bytes 6291460
  5.8 35.7 %copy-start.4 = (bf16[1,8,128,128]{3,2,1,0:T(8,128)(2,1)S(1)}, bf16[1,8,128,128]{3,2,1,0:T(8,128)(2,1)}, u32[]{:S(2)}) copy-start(bf16[1,8,128,128]{3,2,1,0:T(8,128)(2,1)} %param.14) | copy-start | bytes 786436
  5.8 35.7 %copy-start.6 = (bf16[3,256,128]{2,1,0:T(8,128)(2,1)S(1)}, bf16[3,256,128]{2,1,0:T(8,128)(2,1)}, u32[]{:S(2)}) copy-start(bf16[3,256,128]{2,1,0:T(8,128)(2,1)} %down_ref.1) | copy-start | bytes 589828

commit v3 on v2

--- a/solution.py
+++ b/solution.py
@@ -25,13 +25,6 @@
     )
 
 
-def near_first(count):
-    order = [0]
-    for step in range(1, count // 2 + 1):
-        order += [step] if step == count - step else [step, count - step]
-    return order
-
-
 def greet(devices):
     barrier = pltpu.get_barrier_semaphore()
     for device in devices:
@@ -41,6 +34,7 @@
 
 def encode_kernel(tiles, x_hbm, w_ref, fc_hbm, out_ref, x_ref, fc_ref, w_all, acc, ld, z_s, z_r, xy_s, xy_r, dg_s, dg_r, pt_s, pt_r):
     zs = tiles // CORES
+    far = zs // 2
     rows = w_ref.shape[0]
     half = rows // 2
     sx = lax.axis_index("section")
@@ -48,18 +42,17 @@
     t = lax.axis_index("tile")
     z, c = t // CORES, t % CORES
     ox, oy, oc = 1 - sx, 1 - sy, 1 - c
+    oz = z + 1 - 2 * (z % 2)
     partner = {"tile": z * CORES + oc}
-    xn, yn = {"section": ox}, {"slide": oy}
-
-    def zdev(o):
-        return {"tile": ((z + o) % zs) * CORES + c}
-
-    def at(x, o, core, y, part=None):
-        zz = (z + o) % zs
-        start = ((x * tiles + zz * CORES + core) * 2 + y) * rows
-        if part is None:
-            return w_all.at[pl.ds(pl.multiple_of(start, rows), rows)]
-        return w_all.at[pl.ds(pl.multiple_of(start + part * half, half), half)]
+    xn, yn, zn = {"section": ox}, {"slide": oy}, {"tile": oz * CORES + c}
+    places = [z] + [(z + 2 * j) % zs for j in range(1, far)] + [oz] + [(oz + 2 * j) % zs for j in range(1, far)]
+
+    def zdev(j):
+        return {"tile": ((z + 2 * j) % zs) * CORES + c}
+
+    def at(x, m, core, y, k):
+        start = ((x * tiles + places[m] * CORES + core) * 2 + y) * rows + k * half
+        return w_all.at[pl.ds(pl.multiple_of(start, half), half)]
 
     started = []
 
@@ -72,85 +65,88 @@
         remote(dst, dst, ss, rs, device).wait_recv()
 
     loads = [pltpu.make_async_copy(x_hbm, x_ref, ld.at[0]), pltpu.make_async_copy(fc_hbm, fc_ref, ld.at[1])]
+    wait = greet([partner, xn, yn, zn] + [zdev(j) for j in range(1, far)])
     for load in loads:
         load.start()
-    wait = greet([partner, xn, yn] + [zdev(o) for o in range(1, zs)])
     start = ((sx * tiles + t) * 2 + sy) * rows
     w_all[pl.ds(pl.multiple_of(start, rows), rows)] = w_ref[...]
     wait()
 
-    order = near_first(zs)
-    for o in order[1:]:
-        go(w_ref, at(sx, 0, c, sy), z_s.at[o], z_r.at[o], zdev(o))
-
-    def line(o):
-        src = w_ref if o == 0 else at(sx, o, c, sy)
-        if o:
-            arrived(src, z_s.at[0], z_r.at[zs - o], zdev(o))
-        here = at(sx, o, c, sy)
-        go(src, here, xy_s.at[0, o], xy_r.at[0, o], xn)
-        go(src, here, xy_s.at[1, o], xy_r.at[1, o], yn)
-        go(src, here, pt_s.at[0, o], pt_r.at[0, o], partner)
-
-    def cross(o):
-        ref = at(ox, o, c, sy)
-        arrived(ref, xy_s.at[0, o], xy_r.at[0, o], xn)
-        part = at(ox, o, c, sy, 0)
-        go(part, part, dg_s.at[0, o], dg_r.at[0, o], yn)
-        go(ref, ref, pt_s.at[1, o], pt_r.at[1, o], partner)
-        ref = at(sx, o, c, oy)
-        arrived(ref, xy_s.at[1, o], xy_r.at[1, o], yn)
-        part = at(sx, o, c, oy, 1)
-        go(part, part, dg_s.at[1, o], dg_r.at[1, o], xn)
-        go(ref, ref, pt_s.at[2, o], pt_r.at[2, o], partner)
-
-    def corner(o):
-        for k, device in enumerate((yn, xn)):
-            part = at(ox, o, c, oy, k)
-            arrived(part, dg_s.at[k, o], dg_r.at[k, o], device)
-            go(part, part, pt_s.at[3 + k, o], pt_r.at[3 + k, o], partner)
+    def own(k):
+        return w_ref.at[pl.ds(k * half, half)]
+
+    for k in range(2):
+        for j in range(1, far):
+            go(own(k), at(sx, 0, c, sy, k), z_s.at[j, k], z_r.at[j, k], zdev(j))
+    for k in range(2):
+        go(own(k), at(sx, 0, c, sy, k), z_s.at[far, k], z_r.at[far, k], zn)
+
+    def line(m, k):
+        here = at(sx, m, c, sy, k)
+        src = here if m else own(k)
+        if 0 < m < far:
+            arrived(here, z_s.at[0, k], z_r.at[far - m, k], zdev(m))
+        elif m:
+            arrived(here, z_s.at[0, k], z_r.at[m, k], zn)
+        go(src, here, xy_s.at[0, m, k], xy_r.at[0, m, k], xn)
+        go(src, here, xy_s.at[1, m, k], xy_r.at[1, m, k], yn)
+        if 0 < m < far:
+            go(src, here, z_s.at[far + m, k], z_r.at[far + m, k], zn)
+        go(src, here, pt_s.at[0, m, k], pt_r.at[0, m, k], partner)
+
+    def cross(m, k):
+        for kind, device, other, ref in (
+            (0, xn, yn, at(ox, m, c, sy, k)),
+            (1, yn, xn, at(sx, m, c, oy, k)),
+        ):
+            arrived(ref, xy_s.at[kind, m, k], xy_r.at[kind, m, k], device)
+            if k == kind:
+                go(ref, ref, dg_s.at[m, k], dg_r.at[m, k], other)
+            go(ref, ref, pt_s.at[1 + kind, m, k], pt_r.at[1 + kind, m, k], partner)
+
+    def corner(m, k):
+        ref = at(ox, m, c, oy, k)
+        arrived(ref, dg_s.at[m, k], dg_r.at[m, k], (yn, xn)[k])
+        go(ref, ref, pt_s.at[3, m, k], pt_r.at[3, m, k], partner)
 
     depth = CORES * 2 * rows
-
-    def multiply(o, first):
-        refs = [at(sx, o, oc, sy), at(ox, o, oc, sy), at(sx, o, oc, oy), at(ox, o, oc, oy, 0), at(ox, o, oc, oy, 1)]
-        for k, ref in enumerate(refs):
-            arrived(ref, pt_s.at[k, o], pt_r.at[k, o], partner)
-        cols = [((x * zs) + (z + o) % zs) * depth for x in (sx, ox)]
-        slabs = [pl.ds(pl.multiple_of(s, depth), depth) for s in cols]
-        tall = x_ref.shape[0] // 4
+    tall = x_ref.shape[0] // 4
+
+    def multiply(m):
+        for k in range(2):
+            for kind, (x, y) in enumerate(((sx, sy), (ox, sy), (sx, oy), (ox, oy))):
+                arrived(at(x, m, oc, y, k), pt_s.at[kind, m, k], pt_r.at[kind, m, k], partner)
+        slabs = [pl.ds(pl.multiple_of((x * zs + places[m]) * depth, depth), depth) for x in (sx, ox)]
 
         def body(i, carry):
             strip = pl.ds(pl.multiple_of(i * tall, tall), tall)
             total = jnp.dot(x_ref[strip, slabs[0]], w_all[slabs[0], :], preferred_element_type=F32)
             total += jnp.dot(x_ref[strip, slabs[1]], w_all[slabs[1], :], preferred_element_type=F32)
-            acc[strip, :] = total if first else acc[strip, :] + total
+            if m:
+                total += acc[strip, :]
+            if m < zs - 1:
+                acc[strip, :] = total
+            else:
+                enc = jnp.maximum(total, 0.0).astype(BF)
+                out_ref[strip, :] = jnp.dot(enc, fc_ref[...], preferred_element_type=F32)
             return carry
 
         lax.fori_loop(0, 4, body, 0)
 
-    for step in range(zs + 3):
-        if step < zs:
-            line(order[step])
-        if 0 <= step - 1 < zs:
-            cross(order[step - 1])
-        if 0 <= step - 2 < zs:
-            corner(order[step - 2])
-        if step == 3:
-            loads[0].wait()
-        if 0 <= step - 3 < zs:
-            multiply(order[step - 3], step == 3)
-
-    tall = x_ref.shape[0] // 4
-    loads[1].wait()
-
-    def finish(i, carry):
-        strip = pl.ds(pl.multiple_of(i * tall, tall), tall)
-        enc = jnp.maximum(acc[strip, :], 0.0).astype(BF)
-        out_ref[strip, :] = jnp.dot(enc, fc_ref[...], preferred_element_type=F32)
-        return carry
-
-    lax.fori_loop(0, 4, finish, 0)
+    steps = [(m, k) for m in range(zs) for k in range(2)]
+    count = len(steps)
+    for step in range(count + 5):
+        if step < count:
+            line(*steps[step])
+        if 0 <= step - 2 < count:
+            cross(*steps[step - 2])
+        if 0 <= step - 4 < count:
+            corner(*steps[step - 4])
+        if step == 5:
+            for load in loads:
+                load.wait()
+        if 0 <= step - 5 < count and steps[step - 5][1]:
+            multiply(steps[step - 5][0])
     for copy in started:
         copy.wait_send()
 
@@ -172,17 +168,17 @@
             pltpu.VMEM((rows.shape[1], w_proj.shape[1]), BF),
             pltpu.VMEM((rows.shape[0], w_proj.shape[1]), F32),
             dma((2,)),
-            dma((zs,)),
-            dma((zs,)),
-            dma((2, zs)),
-            dma((2, zs)),
-            dma((2, zs)),
-            dma((2, zs)),
-            dma((5, zs)),
-            dma((5, zs)),
+            dma((zs, 2)),
+            dma((zs, 2)),
+            dma((2, zs, 2)),
+            dma((2, zs, 2)),
+            dma((zs, 2)),
+            dma((zs, 2)),
+            dma((4, zs, 2)),
+            dma((4, zs, 2)),
         ],
         compiler_params=pltpu.CompilerParams(
-            collective_id=0, has_side_effects=True, vmem_limit_bytes=40 << 20
+            collective_id=0, has_side_effects=True, vmem_limit_bytes=61 << 20
         ),
         name="encode",
     )(rows, w_proj, w_fc)

time: 134 us -> 131 us (0.978)
  local copies, waits for them, and re-layouts: 5.3 us -> 2.3 us
    unnamed x17 -> x13, local copies, waits for them, and re-layouts: 4.76 us -> 1.76 us
where the time goes in v3:
time: 131 us; the launch traced here: 130 us
  Pallas kernels  127 us (97%)
  local copies, waits for them, and re-layouts  2.3 us (2%)
    pallas_call x1, Pallas kernels, graph(): pl.pallas_call(functools.partial(hops_kernel, tiles, cap, parts), out_sha...  90.6 us
    pallas_call x1, Pallas kernels, encode(): pl.pallas_call(functools.partial(encode_kernel, tiles), out_shape=jax.Sha...  36.2 us

profile of v3, /device:TPU:0, one launch (start us, length us, event | category | flops | bytes accessed | tf_op | source)
XLA Modules:
  0.0 130.5 jit_solution(14632057847235589961)
XLA Ops:
  0.0 0.0 copy-start
  0.0 0.0 copy-start.1
  0.0 0.0 copy-start.3
  0.0 0.0 copy-start.4
  0.0 0.9 iota_compare_fusion.2
  0.9 0.1 lt.47
  1.0 0.0 copy-done
  1.0 0.1 constant_dynamic-slice_fusion
  1.1 0.1 copy.12
  1.2 0.1 eq.52
  1.2 0.2 convert_reduce_fusion
  1.4 0.1 fusion
  1.5 0.1 select_reduce_fusion
  1.7 0.1 copy.13
  1.8 0.1 add.26.list_ref
  1.9 36.2 %encode.1.state_ref = f32[1024,128]{1,0:T(8,128)} custom-call(bf16[1024,2048]{1,0:T(8,128)(2,1)} %bitcast.8, bf16[64,1024]{1,0:T(8,128)(2,1)} %w_ref.1, bf16[1024,128]{1,0:T(8,128)(2,1)} %fc_hbm.1), custom_call_target="tpu_custom_call" | custom-call | tf_op jit(solution)/shard_map/encode/pallas_call | solution.py:160
  38.1 0.0 copy-done.1
  38.1 0.0 copy-done.3
  38.1 0.0 copy-done.5
  38.1 0.0 copy-done.4
  38.1 0.0 copy-start.2
  38.1 1.0 copy-done.2
  39.2 90.6 %hops.1 = bf16[1024,128]{1,0:T(8,128)(2,1)S(1)} custom-call(s32[512]{0:T(512)S(1)} %add.26.list_ref, f32[1024,128]{1,0:T(8,128)S(1)} %copy-done.2, bf16[8,8,128,128]{3,2,1,0:T(8,128)(2,1)S(1)} %bitcast.5, bf16[8,128,128]{2,1,0:T(8,128)(2,1)S(1)} %bitcast.7, bf16[3,128,256]{2,1,0:T(8,128)(2,1)S(1)} %copy-done.4, bf16[3,256,128]{2,1,0:T(8,128)(2,1)S(1)} %copy-done.5), custom_call_target="tpu_custom_call" | custom-call | tf_op jit(solution)/shard_map/hops/pallas_call | solution.py:346
  129.8 0.7 copy.15
  (4 shorter events, 0.0 us)
Async XLA Ops:
  0.0 1.0 copy-start
  0.0 38.1 %copy-start.1 = (bf16[1,8,8,128,128]{4,3,2,1,0:T(8,128)(2,1)S(1)}, bf16[1,8,8,128,128]{4,3,2,1,0:T(8,128)(2,1)}, u32[]{:S(2)}) copy-start(bf16[1,8,8,128,128]{4,3,2,1,0:T(8,128)(2,1)} %param.15) | copy-start | bytes 6291460
  0.0 38.1 %copy-start.3 = (bf16[1,8,128,128]{3,2,1,0:T(8,128)(2,1)S(1)}, bf16[1,8,128,128]{3,2,1,0:T(8,128)(2,1)}, u32[]{:S(2)}) copy-start(bf16[1,8,128,128]{3,2,1,0:T(8,128)(2,1)} %param.14) | copy-start | bytes 786436
  0.0 38.1 %copy-start.5 = (bf16[3,256,128]{2,1,0:T(8,128)(2,1)S(1)}, bf16[3,256,128]{2,1,0:T(8,128)(2,1)}, u32[]{:S(2)}) copy-start(bf16[3,256,128]{2,1,0:T(8,128)(2,1)} %down_ref.1) | copy-start | bytes 589828
  0.0 38.1 %copy-start.4 = (bf16[3,128,256]{2,1,0:T(8,128)(2,1)S(1)}, bf16[3,128,256]{2,1,0:T(8,128)(2,1)}, u32[]{:S(2)}) copy-start(bf16[3,128,256]{2,1,0:T(8,128)(2,1)} %up_ref.1) | copy-start | bytes 589828
  38.1 1.0 copy-start.2

commit v4 on v3

--- a/solution.py
+++ b/solution.py
@@ -135,18 +135,18 @@
 
     steps = [(m, k) for m in range(zs) for k in range(2)]
     count = len(steps)
-    for step in range(count + 5):
+    for step in range(count + 6):
         if step < count:
             line(*steps[step])
-        if 0 <= step - 2 < count:
-            cross(*steps[step - 2])
-        if 0 <= step - 4 < count:
-            corner(*steps[step - 4])
-        if step == 5:
+        if 0 <= step - 3 < count:
+            cross(*steps[step - 3])
+        if 0 <= step - 5 < count:
+            corner(*steps[step - 5])
+        if step == 6:
             for load in loads:
                 load.wait()
-        if 0 <= step - 5 < count and steps[step - 5][1]:
-            multiply(steps[step - 5][0])
+        if 0 <= step - 6 < count and steps[step - 6][1]:
+            multiply(steps[step - 6][0])
     for copy in started:
         copy.wait_send()
 

time: 131 us -> 132 us (level)
  no operation moved by 1% of the time
where the time goes in v4:
time: 132 us
  Pallas kernels  128 us (97%)
  local copies, waits for them, and re-layouts  2.3 us (2%)
    pallas_call x1, Pallas kernels, graph(): pl.pallas_call(functools.partial(hops_kernel, tiles, cap, parts), out_sha...  90.8 us
    pallas_call x1, Pallas kernels, encode(): pl.pallas_call(functools.partial(encode_kernel, tiles), out_shape=jax.Sha...  37.2 us

profile of v4, /device:TPU:0, one launch (start us, length us, event | category | flops | bytes accessed | tf_op | source)
XLA Modules:
  0.0 131.7 jit_solution(9518606212574540064)
XLA Ops:
  0.0 0.0 copy-start
  0.0 0.0 copy-start.1
  0.0 0.0 copy-start.5
  0.0 0.0 copy-start.4
  0.0 0.9 iota_compare_fusion.2
  0.9 0.1 lt.47
  1.0 0.0 copy-done
  1.0 0.1 constant_dynamic-slice_fusion
  1.1 0.1 copy.12
  1.2 0.1 eq.52
  1.2 0.2 convert_reduce_fusion
  1.4 0.1 fusion
  1.5 0.1 select_reduce_fusion
  1.7 0.1 copy.13
  1.8 0.1 add.26.list_ref
  1.9 37.2 %encode.1.state_ref = f32[1024,128]{1,0:T(8,128)} custom-call(bf16[1024,2048]{1,0:T(8,128)(2,1)} %bitcast.8, bf16[64,1024]{1,0:T(8,128)(2,1)} %w_ref.1, bf16[1024,128]{1,0:T(8,128)(2,1)} %fc_hbm.1), custom_call_target="tpu_custom_call" | custom-call | tf_op jit(solution)/shard_map/encode/pallas_call | solution.py:160
  39.1 0.0 copy-done.1
  39.1 0.0 copy-done.3
  39.1 0.0 copy-done.5
  39.1 0.0 copy-done.4
  39.1 0.0 copy-start.2
  39.1 1.0 copy-done.2
  40.2 90.8 %hops.1 = bf16[1024,128]{1,0:T(8,128)(2,1)S(1)} custom-call(s32[512]{0:T(512)S(1)} %add.26.list_ref, f32[1024,128]{1,0:T(8,128)S(1)} %copy-done.2, bf16[8,8,128,128]{3,2,1,0:T(8,128)(2,1)S(1)} %bitcast.5, bf16[8,128,128]{2,1,0:T(8,128)(2,1)S(1)} %bitcast.7, bf16[3,128,256]{2,1,0:T(8,128)(2,1)S(1)} %copy-done.4, bf16[3,256,128]{2,1,0:T(8,128)(2,1)S(1)} %copy-done.5), custom_call_target="tpu_custom_call" | custom-call | tf_op jit(solution)/shard_map/hops/pallas_call | solution.py:346
  131.0 0.7 copy.15
  (4 shorter events, 0.0 us)
Async XLA Ops:
  0.0 1.0 copy-start
  0.0 39.1 %copy-start.1 = (bf16[1,8,8,128,128]{4,3,2,1,0:T(8,128)(2,1)S(1)}, bf16[1,8,8,128,128]{4,3,2,1,0:T(8,128)(2,1)}, u32[]{:S(2)}) copy-start(bf16[1,8,8,128,128]{4,3,2,1,0:T(8,128)(2,1)} %param.15) | copy-start | bytes 6291460
  0.0 39.1 %copy-start.3 = (bf16[1,8,128,128]{3,2,1,0:T(8,128)(2,1)S(1)}, bf16[1,8,128,128]{3,2,1,0:T(8,128)(2,1)}, u32[]{:S(2)}) copy-start(bf16[1,8,128,128]{3,2,1,0:T(8,128)(2,1)} %param.14) | copy-start | bytes 786436
  0.0 39.1 %copy-start.5 = (bf16[3,256,128]{2,1,0:T(8,128)(2,1)S(1)}, bf16[3,256,128]{2,1,0:T(8,128)(2,1)}, u32[]{:S(2)}) copy-start(bf16[3,256,128]{2,1,0:T(8,128)(2,1)} %down_ref.1) | copy-start | bytes 589828
  0.0 39.1 %copy-start.4 = (bf16[3,128,256]{2,1,0:T(8,128)(2,1)S(1)}, bf16[3,128,256]{2,1,0:T(8,128)(2,1)}, u32[]{:S(2)}) copy-start(bf16[3,128,256]{2,1,0:T(8,128)(2,1)} %up_ref.1) | copy-start | bytes 589828
  39.1 1.0 copy-start.2
